TPU v7x, 128 devices: a whole 4x4x4 slice. The times are simulated.
128 devices in a mesh: dp: 16 (over y, z_hi, core), fsdp: 8 (over z_lo, x).
Axes of the slice: x: 4, y: 4, z: 4 (z_hi: 2, z_lo: 2; z = z_hi * 2 + z_lo), core: 2. Of those that a mesh axis runs over, the one named last changes fastest.
Arguments:
- pooled: bfloat16 [16384, 256, 128], P(None, ('dp', 'fsdp')), may hold values from -6 to 6
- feature_order: int32 [256], replicated, may hold values from 0 to 255, each once
- fm_proj: bfloat16 [2, 256, 16], replicated, may hold values from -0.375 to 0.375
- fm_gain: float32 [2, 4096], replicated, may hold values from 0.1 to 1.9
- mlp_weight: bfloat16 [2, 4096, 2048], P(None, None, 'fsdp'), may hold values from -0.09375 to 0.09375
- lcb_weight: bfloat16 [2, 240, 256], replicated, may hold values from -0.375 to 0.375
- out_gain: float32 [2, 128], replicated, may hold values from 0.1 to 1.9
Outputs:
- layer_out: bfloat16 [16384, 256, 128], P(('dp', 'fsdp'))
Inputs may be any that keep to these rules, and one draw needn't show every extreme that they name: feature_order names every feature exactly once.
All inputs are finite; a program needn't handle non-finite values.
Results may differ from a plain program's by a relative error of at most 0.0051.
Values may be sent and summed in bfloat16 or wider, within the bound.
A program may use at most 192 MiB of HBM per device.

v0:
```python
import jax
import jax.numpy as jnp
from jax import lax
from jax.sharding import PartitionSpec as P

N = 256
D = 128
K = 16
NF = 16
LAYERS = 2


def layer_norm(values, gain):
    center = jnp.mean(values, axis=-1, keepdims=True)
    spread = jnp.mean((values - center) ** 2, axis=-1, keepdims=True)
    return (values - center) * lax.rsqrt(spread + 1e-05) * gain


def body(pooled, feature_order, fm_proj, fm_gain, mlp_weight, lcb_weight, out_gain):
    feature_slot = jnp.argsort(feature_order)
    owned_rows = lax.all_to_all(pooled, ("dp", "fsdp"), split_axis=0, concat_axis=1, tiled=True)
    features = jnp.take(owned_rows, feature_slot, axis=1)
    sample_rows = features.shape[0]
    for layer_index in range(LAYERS):
        projected = jnp.einsum(
            "bnd,nk->bdk", features, fm_proj[layer_index], preferred_element_type=jnp.float32
        ).astype(jnp.bfloat16)
        interaction = jnp.einsum(
            "bnd,bdk->bnk", features, projected, preferred_element_type=jnp.float32
        )
        flattened = interaction.reshape(sample_rows, N * K)
        normed = layer_norm(flattened, fm_gain[layer_index]).astype(jnp.bfloat16)
        weight_shard = mlp_weight[layer_index]
        local_cols = jnp.dot(
            lax.all_gather(normed, "fsdp", axis=0, tiled=True),
            weight_shard,
            preferred_element_type=jnp.float32,
        ).astype(jnp.bfloat16)
        fm_out = lax.all_to_all(local_cols, "fsdp", split_axis=0, concat_axis=1, tiled=True)
        fm_out = fm_out.reshape(sample_rows, NF, D)
        lcb_out = jnp.einsum(
            "ln,bnd->bld", lcb_weight[layer_index], features, preferred_element_type=jnp.float32
        )
        combined = jnp.concatenate([fm_out.astype(jnp.float32), lcb_out], axis=1) + features.astype(
            jnp.float32
        )
        features = layer_norm(combined, out_gain[layer_index]).astype(jnp.bfloat16)
    return features


def solution(mesh):
    placed = (P(None, ("dp", "fsdp"), None), P(), P(), P(), P(None, None, "fsdp"), P(), P())
    return jax.shard_map(
        body, mesh=mesh, in_specs=placed, out_specs=P(("dp", "fsdp"), None, None), check_vma=False
    )
```

profile of v0, /device:TPU:32, one launch (start us, length us, event | category | flops | bytes accessed | tf_op | source)
XLA Modules:
  0.0 536.3 jit_solution(16761496204406844374)
XLA Ops:
  6.5 10.7 %all-to-all-start = ((bf16[16384,2,128]{2,1,0:T(2,128)(2,1)}), bf16[16384,2,128]{2,1,0:T(2,128)(2,1)}, u32[]{:S(2)}, u32[]{:S(2)}) async-start(bf16[16384,2,128]{2,1,0:T(2,128)(2,1)} %param.7), calls=%async_computation | async-start | bytes 16777216 | tf_op jit(solution)/shard_map/all_to_all | solution.py:21
  17.3 3.2 sort.17
  20.5 101.4 %all-to-all-done = bf16[16384,2,128]{2,1,0:T(2,128)(2,1)} async-done(((bf16[16384,2,128]{2,1,0:T(2,128)(2,1)}), bf16[16384,2,128]{2,1,0:T(2,128)(2,1)}, u32[]{:S(2)}, u32[]{:S(2)}) %all-to-all-start) | async-done | bytes 8388640 | tf_op jit(solution)/shard_map/all_to_all | solution.py:21
  121.9 7.8 %copy.22 = bf16[16384,2,128]{2,0,1:T(8,128)(2,1)} copy(bf16[16384,2,128]{2,1,0:T(2,128)(2,1)} %all-to-all-done) | data formatting | bytes 16777216 | tf_op jit(solution)/shard_map/all_to_all | solution.py:21
  129.7 10.3 %copy.23 = bf16[128,128,2,128]{3,0,2,1:T(8,128)(2,1)} copy(bf16[128,128,2,128]{3,0,1,2:T(8,128)(2,1)} %bitcast.100) | data formatting | bytes 16777216 | tf_op jit(solution)/shard_map/all_to_all | solution.py:21
  140.1 12.3 %gather_fusion = bf16[256,128,128]{2,1,0:T(8,128)(2,1)} fusion(bf16[128,256,128]{2,0,1:T(8,128)(2,1)} %bitcast.99, s32[1024]{0:T(1024)S(1)} %pad_clamp_fusion), kind=kCustom, calls=%fused_computation | custom fusion | bytes 16778240 | tf_op jit(solution)/shard_map/jit(_take)/gather | solution.py:22
  152.4 20.8 %fusion.44 = (f32[128]{0:T(128)S(1)}, f32[128,256,16]{1,2,0:T(8,128)}) fusion(bf16[2,256,16]{1,2,0:T(8,128)(2,1)S(1)} %copy-done.4, bf16[256,128,128]{2,1,0:T(8,128)(2,1)} %gather_fusion, pred[256]{0:T(512)(128)(4,1)S(1)} %compare_and_fusion), kind=kOutput, calls=%fused_computation.62 | convolution fusion | flops 277610368 | bytes 18884096 | tf_op jit(solution)/shard_map/bnd,bdk->bnk/dot_general | solution.py:28
  175.7 3.5 multiply_reduce_fusion.3
  181.0 102.7 %all-gather.3.cloned.1.call-done = bf16[1024,4096]{0,1:T(8,128)(2,1)} async-done(((bf16[128,4096]{0,1:T(8,128)(2,1)}), bf16[1024,4096]{0,1:T(8,128)(2,1)}) %all-gather.3.cloned.1.call-update) | async-done | bytes 8388624 | tf_op jit(solution)/shard_map/all_gather | solution.py:35
  283.6 7.1 %fusion.17 = bf16[1024,256]{1,0:T(8,128)(2,1)} fusion(bf16[1024,4096]{0,1:T(8,128)(2,1)} %all-gather.3.cloned.1.call-done, bf16[2,4096,256]{2,1,0:T(8,128)(2,1)} %param.11), kind=kOutput, calls=%fused_computation.31 | convolution fusion | flops 2147745792 | bytes 11010048 | tf_op jit(solution)/shard_map/dot_general | solution.py:34
  290.8 5.2 all-to-all-start.1
  296.0 15.3 %convolution_bitcast_fusion.1 = f32[128,240,128]{2,1,0:T(8,128)} fusion(bf16[2,240,256]{2,1,0:T(8,128)(2,1)S(1)} %copy-done.2, bf16[256,128,128]{2,1,0:T(8,128)(2,1)} %gather_fusion, pred[256]{0:T(512)(128)(4,1)S(1)} %compare_and_fusion), kind=kOutput, calls=%fused_computation.8 | convolution fusion | flops 2017460224 | bytes 24240640 | tf_op jit(solution)/shard_map/ln,bnd->bld/dot_general | solution.py:41
  315.3 14.1 %fusion.30 = f32[128,256]{1,0:T(8,128)S(1)} fusion(f32[128,240,128]{2,1,0:T(8,128)} %convolution_bitcast_fusion.1, f32[128,16,128]{2,1,0:T(8,128)} %reshape.87, bf16[256,128,128]{2,1,0:T(8,128)(2,1)} %gather_fusion, pred[256]{0:T(512)(128)(4,1)S(1)} %compare_and_fusion), kind=kLoop, calls=%fused_computation.39 | loop fusion | flops 20938752 | bytes 25297152 | tf_op jit(solution)/shard_map/reduce_sum | solution.py:14
  329.4 11.8 %multiply_reduce_fusion.1 = f32[128,256]{1,0:T(8,128)S(1)} fusion(f32[128,256]{1,0:T(8,128)S(1)} %broadcast_multiply_fusion.1, f32[128,240,128]{2,1,0:T(8,128)S(1)} %bitcast.98, f32[128,16,128]{2,1,0:T(8,128)S(1)} %copy-done.1, bf16[256,128,128]{2,1,0:T(8,128)(2,1)} %gather_fusion, pred[256]{0:T(512)(128)(4,1)S(1)} %compare_and_fusion), kind=kLoop, calls=%fused_computation.6 | loop fusion | flops 29327360 | bytes 25428224 | tf_op jit(solution)/shard_map/reduce_sum | solution.py:15
  341.3 13.2 %multiply_convert_fusion.1 = bf16[128,256,128]{2,1,0:T(8,128)(2,1)} fusion(f32[128]{0:T(128)S(1)} %get-tuple-element.9, f32[128,256]{1,0:T(8,128)S(1)} %add_rsqrt_fusion.1, f32[128,256]{1,0:T(8,128)S(1)} %broadcast_multiply_fusion.1, f32[128,240,128]{2,1,0:T(8,128)S(1)} %bitcast.98, f32[128,16,128]{2,1,0:T(8,128)S(1)} %copy-done.1, ...), kind=kLoop, calls=%fused_computation.5 | loop fusion | flops 33554432 | bytes 33817344 | tf_op jit(solution)/shard_map/convert_element_type | solution.py:47
  354.5 9.4 %fusion.49 = (f32[128]{0:T(128)S(1)}, f32[128,256,16]{1,2,0:T(8,128)S(1)}) fusion(bf16[128,256,128]{2,1,0:T(8,128)(2,1)} %multiply_convert_fusion.1, bf16[2,256,16]{1,2,0:T(8,128)(2,1)S(1)} %copy-done.4), kind=kOutput, calls=%fused_computation.63 | convolution fusion | flops 269221760 | bytes 18883072 | tf_op jit(solution)/shard_map/bnd,bdk->bnk/dot_general | solution.py:28
  368.0 2.8 fusion.9
  370.8 99.3 %all-gather.5.cloned.1.call-done = bf16[1024,4096]{0,1:T(8,128)(2,1)} async-done(((bf16[128,4096]{0,1:T(8,128)(2,1)}), bf16[1024,4096]{0,1:T(8,128)(2,1)}) %all-gather.5.cloned.1.call-update) | async-done | bytes 8388624 | tf_op jit(solution)/shard_map/all_gather | solution.py:35
  470.2 7.2 %fusion.20 = bf16[1024,256]{1,0:T(8,128)(2,1)} fusion(bf16[1024,4096]{0,1:T(8,128)(2,1)} %all-gather.5.cloned.1.call-done, bf16[2,4096,256]{2,1,0:T(8,128)(2,1)} %param.11), kind=kOutput, calls=%fused_computation.32 | convolution fusion | flops 2147745792 | bytes 11010048 | tf_op jit(solution)/shard_map/dot_general | solution.py:34
  477.3 5.4 %all-to-all-start.2 = ((bf16[8,128,256]{2,1,0:T(8,128)(2,1)}), bf16[8,128,256]{2,1,0:T(8,128)(2,1)S(1)}, u32[]{:S(2)}, u32[]{:S(2)}) async-start(bf16[8,128,256]{2,1,0:T(8,128)(2,1)} %bitcast.20), calls=%async_computation.2 | async-start | bytes 1048576 | tf_op jit(solution)/shard_map/all_to_all | solution.py:39
  482.8 11.1 %convolution_bitcast_fusion = f32[128,240,128]{2,1,0:T(8,128)} fusion(bf16[128,256,128]{2,1,0:T(8,128)(2,1)} %multiply_convert_fusion.1, bf16[2,240,256]{2,1,0:T(8,128)(2,1)S(1)} %copy-done.2), kind=kOutput, calls=%fused_computation.7 | convolution fusion | flops 2013265920 | bytes 24240128 | tf_op jit(solution)/shard_map/ln,bnd->bld/dot_general | solution.py:41
  494.7 11.9 %fusion.29 = f32[128,256]{1,0:T(8,128)S(1)} fusion(bf16[128,256,128]{2,1,0:T(8,128)(2,1)} %multiply_convert_fusion.1, f32[128,240,128]{2,1,0:T(8,128)} %convolution_bitcast_fusion, f32[128,16,128]{2,1,0:T(8,128)S(1)} %reshape.88), kind=kLoop, calls=%fused_computation.38 | loop fusion | flops 16744448 | bytes 25296896 | tf_op jit(solution)/shard_map/reduce_sum | solution.py:14
  507.1 11.2 %multiply_reduce_fusion = f32[128,256]{1,0:T(8,128)S(1)} fusion(f32[128,256]{1,0:T(8,128)S(1)} %broadcast_multiply_fusion, bf16[128,256,128]{2,1,0:T(8,128)(2,1)} %multiply_convert_fusion.1, f32[128,240,128]{2,1,0:T(8,128)S(1)} %copy-done, f32[128,16,128]{2,1,0:T(8,128)S(1)} %reshape.88), kind=kLoop, calls=%fused_computation.4 | loop fusion | flops 25133056 | bytes 25427968 | tf_op jit(solution)/shard_map/reduce_sum | solution.py:15
  518.4 10.9 %multiply_convert_fusion = bf16[128,256,128]{2,1,0:T(8,128)(2,1)} fusion(f32[128]{0:T(128)S(1)} %get-tuple-element.10, f32[128,256]{1,0:T(8,128)S(1)} %add_rsqrt_fusion, f32[128,256]{1,0:T(8,128)S(1)} %broadcast_multiply_fusion, bf16[128,256,128]{2,1,0:T(8,128)(2,1)S(1)} %bitcast.96, f32[128,240,128]{2,1,0:T(8,128)S(1)} %copy-done, ...), kind=kLoop, calls=%fused_computation.3 | loop fusion | flops 29360128 | bytes 33817088 | tf_op jit(solution)/shard_map/convert_element_type | solution.py:47
  (58 shorter events, 13.9 us)
Async XLA Ops:
  6.5 10.8 %copy-start.5 = (s32[256]{0:T(256)S(1)}, s32[256]{0:T(256)}, u32[]{:S(2)}) copy-start(s32[256]{0:T(256)} %param.8) | copy-start | bytes 3076
  6.5 14.0 %copy-start.3 = (f32[2,4096]{1,0:T(2,128)S(1)}, f32[2,4096]{1,0:T(2,128)}, u32[]{:S(2)}) copy-start(f32[2,4096]{1,0:T(2,128)} %param.10) | copy-start | bytes 98308
  6.5 115.4 %all-to-all-start = ((bf16[16384,2,128]{2,1,0:T(2,128)(2,1)}), bf16[16384,2,128]{2,1,0:T(2,128)(2,1)}, u32[]{:S(2)}, u32[]{:S(2)}) async-start(bf16[16384,2,128]{2,1,0:T(2,128)(2,1)} %param.7), calls=%async_computation | async-start | bytes 16777216 | tf_op jit(solution)/shard_map/all_to_all | solution.py:21
  17.2 266.4 %all-gather.3.cloned.1.call-start = ((), (), s32[]{:S(2)}) async-start(), calls=%async_computation.3 | async-start | bytes 9437184 | tf_op jit(solution)/shard_map/all_gather | solution.py:35
  140.1 12.3 %copy-start.4 = (bf16[2,256,16]{1,2,0:T(8,128)(2,1)S(1)}, bf16[2,256,16]{1,2,0:T(8,128)(2,1)}, u32[]{:S(2)}) copy-start(bf16[2,256,16]{1,2,0:T(8,128)(2,1)} %param.9) | copy-start | bytes 49156
  173.2 7.8 %copy-start.6 = (f32[2,128]{1,0:T(2,128)S(1)}, f32[2,128]{1,0:T(2,128)}, u32[]{:S(2)}) copy-start(f32[2,128]{1,0:T(2,128)} %param.13) | copy-start | bytes 3076
  179.2 116.8 %copy-start.2 = (bf16[2,240,256]{2,1,0:T(8,128)(2,1)S(1)}, bf16[2,240,256]{2,1,0:T(8,128)(2,1)}, u32[]{:S(2)}) copy-start(bf16[2,240,256]{2,1,0:T(8,128)(2,1)} %param.12) | copy-start | bytes 737284
  290.8 20.5 %all-to-all-start.1 = ((bf16[8,128,256]{2,1,0:T(8,128)(2,1)}), bf16[8,128,256]{2,1,0:T(8,128)(2,1)S(1)}, u32[]{:S(2)}, u32[]{:S(2)}) async-start(bf16[8,128,256]{2,1,0:T(8,128)(2,1)} %bitcast.9), calls=%async_computation.1 | async-start | bytes 1048576 | tf_op jit(solution)/shard_map/all_to_all | solution.py:39
  296.0 174.2 %all-gather.5.cloned.1.call-start = ((), (), s32[]{:S(2)}) async-start(), calls=%async_computation.4 | async-start | bytes 9437184 | tf_op jit(solution)/shard_map/all_gather | solution.py:35
  311.4 18.0 %slice-start.2 = ((s8[15728640]{0:T(1024)(128)(4,1)}), s8[3145728]{0:T(1024)(128)(4,1)S(1)}, s32[]{:S(2)}) async-start(s8[15728640]{0:T(1024)(128)(4,1)} %bitcast.97), calls=%async_computation.7 | async-start | bytes 6291456
  315.3 14.1 %slice-start.3 = ((s8[15728640]{0:T(1024)(128)(4,1)}), s8[4194304]{0:T(1024)(128)(4,1)S(1)}, s32[]{:S(2)}) async-start(s8[15728640]{0:T(1024)(128)(4,1)} %bitcast.97), calls=%async_computation.8 | async-start | bytes 8388608
  315.3 14.1 %slice-start.4 = ((s8[15728640]{0:T(1024)(128)(4,1)}), s8[4194304]{0:T(1024)(128)(4,1)S(1)}, s32[]{:S(2)}) async-start(s8[15728640]{0:T(1024)(128)(4,1)} %bitcast.97), calls=%async_computation.9 | async-start | bytes 8388608
  315.3 14.1 %slice-start.5 = ((s8[15728640]{0:T(1024)(128)(4,1)}), s8[4194304]{0:T(1024)(128)(4,1)S(1)}, s32[]{:S(2)}) async-start(s8[15728640]{0:T(1024)(128)(4,1)} %bitcast.97), calls=%async_computation.10 | async-start | bytes 8388608
  315.3 14.1 %copy-start.1 = (f32[128,16,128]{2,1,0:T(8,128)S(1)}, f32[128,16,128]{2,1,0:T(8,128)}, u32[]{:S(2)}) copy-start(f32[128,16,128]{2,1,0:T(8,128)} %reshape.87) | copy-start | bytes 3145732
  477.3 16.6 %all-to-all-start.2 = ((bf16[8,128,256]{2,1,0:T(8,128)(2,1)}), bf16[8,128,256]{2,1,0:T(8,128)(2,1)S(1)}, u32[]{:S(2)}, u32[]{:S(2)}) async-start(bf16[8,128,256]{2,1,0:T(8,128)(2,1)} %bitcast.20), calls=%async_computation.2 | async-start | bytes 1048576 | tf_op jit(solution)/shard_map/all_to_all | solution.py:39
  494.7 12.4 %copy-start = (f32[128,240,128]{2,1,0:T(8,128)S(1)}, f32[128,240,128]{2,1,0:T(8,128)}, u32[]{:S(2)}) copy-start(f32[128,240,128]{2,1,0:T(8,128)} %convolution_bitcast_fusion) | copy-start | bytes 47185924
  494.7 23.6 %slice-start = ((s8[8388608]{0:T(1024)(128)(4,1)}), s8[4194304]{0:T(1024)(128)(4,1)S(1)}, s32[]{:S(2)}) async-start(s8[8388608]{0:T(1024)(128)(4,1)} %bitcast.95), calls=%async_computation.5 | async-start | bytes 8388608
  507.1 11.2 %slice-start.1 = ((s8[8388608]{0:T(1024)(128)(4,1)}), s8[4194304]{0:T(1024)(128)(4,1)S(1)}, s32[]{:S(2)}) async-start(s8[8388608]{0:T(1024)(128)(4,1)} %bitcast.95), calls=%async_computation.6 | async-start | bytes 8388608
Sparse Core Ops, SparseCore 0:
  181.1 102.5 all-gather.2
  371.0 99.1 all-gather.4
where the time goes:
time: 542 us; the launch traced here: 536 us
  waiting for transfers between devices  303 us (56%)
  other arithmetic  86.3 us (16%)
  matrix products  70.9 us (13%)
  local copies, waits for them, and re-layouts  40.4 us (7%)
  starting transfers between devices  21.4 us (4%)
  between operations  13.9 us (3%)
    all_gather x2, waiting for transfers between devices, body(): lax.all_gather(normed, 'fsdp', axis=0, tiled=True)  202 us
    all_to_all x1, waiting for transfers between devices, body(): lax.all_to_all(pooled, ('dp', 'fsdp'), split_axis=0, concat_axis=1, tiled...  101 us
    dot_general x2, matrix products, body(): jnp.einsum('bnd,bdk->bnk', features, projected, preferred_element_type=jn...  30.1 us
    reduce_sum x4, other arithmetic, layer_norm(): spread = jnp.mean((values - center) ** 2, axis=-1, keepdims=True)  28.3 us
    dot_general x2, matrix products, body(): jnp.einsum('ln,bnd->bld', lcb_weight[layer_index], features, preferred_el...  26.4 us
    reduce_sum x2, other arithmetic, layer_norm(): center = jnp.mean(values, axis=-1, keepdims=True)  25.9 us
    convert_element_type x2, other arithmetic, body(): features = layer_norm(combined, out_gain[layer_index]).astype(jnp.bfloat16)  24.1 us
    all_to_all x2, local copies, waits for them, and re-layouts, body(): lax.all_to_all(pooled, ('dp', 'fsdp'), split_axis=0, concat_axis=1, tiled...  18.1 us
  transfers between devices with their start and end apart: 5, of which 3 were waited for; matrix products, arithmetic and copies ran while one was open for 6% of the time, Pallas kernels for 0%

commit v1 on v0

v1 whole, which is shorter than its diff:
```python
import jax
import jax.numpy as jnp
from jax import lax
from jax.experimental import pallas as pl
from jax.experimental.pallas import tpu as pltpu
from jax.sharding import PartitionSpec as P

N = 256
D = 128
K = 16
LAYERS = 2
DEVICES = 128
BLOCK = 128
CHUNKS = 4
STEP = BLOCK // CHUNKS
HALF = K // 2
MESH = pl.DeviceIdType.MESH
F32 = jnp.float32
BF16 = jnp.bfloat16


def position():
    dp, fsdp = lax.axis_index("dp"), lax.axis_index("fsdp")
    y, z_hi, core = dp // 4, lax.rem(dp // 2, 2), lax.rem(dp, 2)
    z_lo, x = fsdp // 4, lax.rem(fsdp, 4)
    return x, y, z_hi * 2 + z_lo, core


def device_at(x, y, z, core):
    x, y, z = lax.rem(x + 4, 4), lax.rem(y + 4, 4), lax.rem(z + 4, 4)
    return {"dp": (y * 2 + z // 2) * 2 + core, "fsdp": lax.rem(z, 2) * 4 + x}


def gather_kernel(rows, shard, out, full, send, arrive, w_send, w_arrive, own, w_own):
    dp, fsdp = lax.axis_index("dp"), lax.axis_index("fsdp")
    me = dp * 8 + fsdp
    x, y, z, core = position()
    z_lo = lax.rem(z, 2)
    barrier = pltpu.get_barrier_semaphore()

    def mesh_of(t):
        return {"dp": t // 8, "fsdp": lax.rem(t, 8)}

    def greet(i, carry):
        pl.semaphore_signal(
            barrier, inc=1, device_id=mesh_of(lax.rem(me + i, DEVICES)), device_id_type=MESH
        )
        return carry

    lax.fori_loop(1, DEVICES, greet, 0)

    base = core * HALF
    mine = base + 4 + y

    def cols(i):
        return pl.ds(pl.multiple_of(i * 256, 256), 256)

    own_copies = []
    for layer in range(LAYERS):
        for j, (first, count) in enumerate(((base, 4), (mine, 1))):
            copy = pltpu.make_async_copy(
                shard.at[layer, pl.ds(first, count)],
                full.at[layer, pl.ds(first, count), :, cols(fsdp)],
                w_own.at[layer, j],
            )
            copy.start()
            own_copies.append(copy)
    pl.semaphore_wait(barrier, DEVICES - 1)

    def push(layer, slot, source, target, device):
        copy = pltpu.make_async_remote_copy(
            src_ref=source,
            dst_ref=target,
            send_sem=w_send.at[layer, slot],
            recv_sem=w_arrive.at[layer, slot],
            device_id=device,
            device_id_type=MESH,
        )
        copy.start()
        return copy

    right = device_at(x + 1, y, z, core)
    left = device_at(x - 1, y, z, core)
    z_up = device_at(x, y, z + 1, core)
    z_down = device_at(x, y, z - 1, core)
    y_up = device_at(x, y + 1, z, core)
    y_down = device_at(x, y - 1, z, core)
    sibling = device_at(x, y, z, 1 - core)
    from_left = z_lo * 4 + lax.rem(x + 3, 4)
    from_right = z_lo * 4 + lax.rem(x + 1, 4)
    top, bottom = pl.ds(0, 128), pl.ds(128, 128)
    started = []

    def x_first(layer):
        many, one = pl.ds(base, 4), pl.ds(mine, 1)
        return [
            push(layer, 0, shard.at[layer, many], full.at[layer, many, :, cols(fsdp)], right),
            push(layer, 1, shard.at[layer, many], full.at[layer, many, :, cols(fsdp)], left),
            push(layer, 2, shard.at[layer, one], full.at[layer, one, :, cols(fsdp)], right),
            push(layer, 3, shard.at[layer, one], full.at[layer, one, :, cols(fsdp)], left),
        ]

    def same(layer, slot, block, device):
        return push(layer, slot, block, block, device)

    def x_second(layer):
        low, high = pl.ds(base, 2), pl.ds(base + 2, 2)
        return [
            same(layer, 4, full.at[layer, low, :, cols(from_left)], right),
            same(layer, 5, full.at[layer, high, :, cols(from_right)], left),
            same(layer, 6, full.at[layer, mine, top, cols(from_left)], right),
            same(layer, 7, full.at[layer, mine, bottom, cols(from_right)], left),
        ]

    def z_step(layer):
        low, high = pl.ds(base, 2), pl.ds(base + 2, 2)
        group = pl.ds(pl.multiple_of(z_lo * 1024, 1024), 1024)
        return [
            same(layer, 8, full.at[layer, low, :, group], z_up),
            same(layer, 9, full.at[layer, high, :, group], z_down),
            same(layer, 10, full.at[layer, mine, top, group], z_up),
            same(layer, 11, full.at[layer, mine, bottom, group], z_down),
        ]

    def y_first(layer):
        four = pl.ds(base, 4)
        return [
            same(layer, 12, full.at[layer, mine], y_up),
            same(layer, 13, full.at[layer, mine], y_down),
            same(layer, 14, full.at[layer, four], sibling),
        ]

    def y_second(layer):
        lower = base + 4 + lax.rem(y + 3, 4)
        upper = base + 4 + lax.rem(y + 1, 4)
        return [
            same(layer, 15, full.at[layer, lower, top], y_up),
            same(layer, 16, full.at[layer, upper, bottom], y_down),
        ]

    def across(layer):
        return [same(layer, 17, full.at[layer, pl.ds(base + 4, 4)], sibling)]

    def exchange(c):
        def send_one(i, carry):
            t = lax.rem(me + i, DEVICES)
            pltpu.make_async_remote_copy(
                src_ref=rows.at[pl.ds(t * BLOCK + c * STEP, STEP)],
                dst_ref=out.at[pl.ds(c * STEP, STEP), pl.ds(pl.multiple_of(2 * me, 2), 2)],
                send_sem=send.at[c],
                recv_sem=arrive.at[c],
                device_id=mesh_of(t),
                device_id_type=MESH,
            ).start()
            return carry

        lax.fori_loop(1, DEVICES, send_one, 0)
        pltpu.make_async_copy(
            rows.at[pl.ds(me * BLOCK + c * STEP, STEP)],
            out.at[pl.ds(c * STEP, STEP), pl.ds(pl.multiple_of(2 * me, 2), 2)],
            own.at[c],
        ).start()

    def arrived(copies):
        for copy in copies:
            copy.wait_recv()

    first = [x_first(0), x_first(1)]
    exchange(0)
    for copy in own_copies:
        copy.wait()
    second = []
    for layer in range(LAYERS):
        arrived(first[layer])
        second.append(x_second(layer))
    exchange(1)
    third = []
    for layer in range(LAYERS):
        arrived(second[layer])
        third.append(z_step(layer))
    exchange(2)
    fourth = []
    for layer in range(LAYERS):
        arrived(third[layer])
        fourth.append(y_first(layer))
    exchange(3)
    fifth = []
    for layer in range(LAYERS):
        arrived(fourth[layer])
        fifth.append(y_second(layer))
    sixth = []
    for layer in range(LAYERS):
        arrived(fifth[layer])
        sixth.append(across(layer))
    for layer in range(LAYERS):
        arrived(sixth[layer])
    for group in first + second + third + fourth + fifth + sixth:
        for copy in group:
            copy.wait_send()

    for c in range(CHUNKS):
        pltpu.make_async_copy(
            rows.at[pl.ds(0, STEP)], out.at[pl.ds(c * STEP, STEP), pl.ds(0, 2)], own.at[c]
        ).wait()
        part = out.at[pl.ds(c * STEP, STEP), pl.ds(0, N - 2)]
        pltpu.make_async_copy(part, part, arrive.at[c]).wait()
        pltpu.make_async_copy(part, part, send.at[c]).wait()


def gather(rows, shard):
    slots = 18
    return pl.pallas_call(
        gather_kernel,
        out_shape=(
            jax.ShapeDtypeStruct((BLOCK, N, D), BF16),
            jax.ShapeDtypeStruct((LAYERS, K, N, 2048), BF16),
        ),
        in_specs=[pl.BlockSpec(memory_space=pl.ANY)] * 2,
        out_specs=[pl.BlockSpec(memory_space=pl.ANY)] * 2,
        scratch_shapes=[
            pltpu.SemaphoreType.DMA((CHUNKS,)),
            pltpu.SemaphoreType.DMA((CHUNKS,)),
            pltpu.SemaphoreType.DMA((LAYERS, slots)),
            pltpu.SemaphoreType.DMA((LAYERS, slots)),
            pltpu.SemaphoreType.DMA((CHUNKS,)),
            pltpu.SemaphoreType.DMA((LAYERS, 2)),
        ],
        compiler_params=pltpu.CompilerParams(collective_id=0, has_side_effects=True),
    )(rows, shard)


def normalized(values, gain):
    center = jnp.mean(values, axis=-1, keepdims=True)
    apart = values - center
    spread = jnp.mean(apart * apart, axis=-1, keepdims=True)
    return (apart * lax.rsqrt(spread + 1e-05) * gain).astype(BF16)


def features_of_block(count, block, order, weights, layer, mixer, gains, out_gain, inter, fm):
    def pair(i, carry):
        a, b = 2 * i, 2 * i + 1
        both = jnp.concatenate([block[a], block[b]], axis=1)
        if order is not None:
            both = jnp.dot(order, both, preferred_element_type=F32).astype(BF16)
        mixed = jnp.dot(mixer[layer], both, preferred_element_type=F32)
        projected = mixed[:K].astype(BF16)
        for s, at in ((a, 0), (b, D)):
            rows = both[:, at : at + D]
            products = lax.dot_general(
                projected[:, at : at + D],
                rows,
                (((1,), (1,)), ((), ())),
                preferred_element_type=F32,
            )
            for half in range(2):
                inter[half, pl.ds(pl.multiple_of(s * K, K), K), :] = products[
                    :, half * D : (half + 1) * D
                ]
            combined = mixed[K:, at : at + D] + rows[K:].astype(F32)
            block[s, :K] = rows[:K]
            block[s, K:] = normalized(combined, out_gain[layer])
        return carry

    lax.fori_loop(0, count // 2, pair, 0)

    def taken(k):
        return jnp.concatenate(
            [inter[half, pl.ds(k, count, stride=K), :] for half in range(2)], axis=1
        )

    total = jnp.zeros((count, N), F32)
    for k in range(K):
        total += taken(k)
    center = jnp.sum(total, axis=-1, keepdims=True) * (1.0 / (N * K))
    squares = jnp.zeros((count, N), F32)
    for k in range(K):
        apart = taken(k) - center
        squares += apart * apart
    scale = lax.rsqrt(jnp.sum(squares, axis=-1, keepdims=True) * (1.0 / (N * K)) + 1e-05)
    width = 512

    def columns(j, carry):
        at = pl.multiple_of(j * width, width)
        made = jnp.zeros((count, width), F32)
        for k in range(K):
            apart = taken(k) - center
            normed = (apart * scale * gains[layer, k : k + 1, :]).astype(BF16)
            made += jnp.dot(
                normed, weights[layer, k, :, pl.ds(at, width)], preferred_element_type=F32
            )
        made = made.astype(BF16).astype(F32)
        for f in range(width // D):
            fm[pl.ds(j * (width // D) + f, count, stride=K), :] = made[:, f * D : (f + 1) * D]
        return carry

    lax.fori_loop(0, 2048 // width, columns, 0)

    def finish(s, carry):
        combined = fm[pl.ds(pl.multiple_of(s * K, K), K), :] + block[s, :K].astype(F32)
        block[s, :K] = normalized(combined, out_gain[layer])
        return carry

    lax.fori_loop(0, count, finish, 0)


def layers_kernel(x, full, slots, mixer, gains, out_gain, out, block, weights, inter, fm, sem):
    take = pltpu.make_async_copy(x, block, sem.at[0])
    take.start()
    loads = []
    for layer in range(LAYERS):
        load = pltpu.make_async_copy(full.at[layer], weights.at[layer], sem.at[1 + layer])
        load.start()
        loads.append(load)
    order = jnp.where(
        lax.broadcasted_iota(jnp.int32, (N, N), 0) == slots[...], 1.0, 0.0
    ).astype(BF16)
    take.wait()
    for layer in range(LAYERS):
        loads[layer].wait()
        features_of_block(
            BLOCK,
            block,
            order if layer == 0 else None,
            weights,
            layer,
            mixer,
            gains,
            out_gain,
            inter,
            fm,
        )
    give = pltpu.make_async_copy(block, out, sem.at[0])
    give.start()
    give.wait()


def layers(x, full, slots, mixer, gains, out_gain):
    vmem = pl.BlockSpec(memory_space=pltpu.VMEM)
    hbm = pl.BlockSpec(memory_space=pl.ANY)
    return pl.pallas_call(
        layers_kernel,
        out_shape=jax.ShapeDtypeStruct((BLOCK, N, D), BF16),
        in_specs=[hbm, hbm, vmem, vmem, vmem, vmem],
        out_specs=hbm,
        scratch_shapes=[
            pltpu.VMEM((BLOCK, N, D), BF16),
            pltpu.VMEM((LAYERS, K, N, 2048), BF16),
            pltpu.VMEM((2, BLOCK * K, D), F32),
            pltpu.VMEM((BLOCK * K, D), F32),
            pltpu.SemaphoreType.DMA((3,)),
        ],
        compiler_params=pltpu.CompilerParams(vmem_limit_bytes=60 << 20),
    )(x, full, slots, mixer, gains, out_gain)


def body(pooled, feature_order, fm_proj, fm_gain, mlp_weight, lcb_weight, out_gain):
    shard = mlp_weight.reshape(LAYERS, N, K, 256).transpose(0, 2, 1, 3)
    gains = fm_gain.reshape(LAYERS, N, K).transpose(0, 2, 1)
    mixer = jnp.concatenate([fm_proj.transpose(0, 2, 1), lcb_weight], axis=1)
    x, full = gather(pooled, shard)
    return layers(
        x, full, feature_order.reshape(1, N), mixer, gains, out_gain.reshape(LAYERS, 1, D)
    )


def solution(mesh):
    placed = (P(None, ("dp", "fsdp"), None), P(), P(), P(), P(None, None, "fsdp"), P(), P())
    return jax.shard_map(
        body, mesh=mesh, in_specs=placed, out_specs=P(("dp", "fsdp"), None, None), check_vma=False
    )
```

time: 542 us -> 389 us (0.72)
  Pallas kernels: 0 us -> 378 us
  waiting for transfers between devices: 303 us -> 0 us
  other arithmetic: 86.3 us -> 1.68 us
  matrix products: 70.9 us -> 0 us
  local copies, waits for them, and re-layouts: 40.4 us -> 7.32 us
  starting transfers between devices: 21.4 us -> 0 us
  between operations: 13.9 us -> 0.02 us
    pallas_call x0 -> x2, Pallas kernels: none -> 378 us  [the longest x1 247 us: gather(): pl.pallas_call(gather_kernel, out_shape=(jax.ShapeDtypeStruct((BLOCK, N,...]
    all_gather x2 -> x0, waiting for transfers between devices: 202 us -> none  [body(): lax.all_gather(normed, 'fsdp', axis=0, tiled=True)]
    all_to_all x3 -> x0, waiting for transfers between devices: 101 us -> none  [the longest x1 101 us: body(): lax.all_to_all(pooled, ('dp', 'fsdp'), split_axis=0, concat_axis=1, tiled...]
    dot_general x6 -> x0, matrix products: 70.9 us -> none  [the longest x2 30.1 us: body(): jnp.einsum('bnd,bdk->bnk', features, projected, preferred_element_type=jn...]
    reduce_sum x6 -> x0, other arithmetic: 54.2 us -> none  [the longest x4 28.3 us: layer_norm(): spread = jnp.mean((values - center) ** 2, axis=-1, keepdims=True)]
    convert_element_type x6 -> x0, other arithmetic: 28.8 us -> none  [the longest x2 24.1 us: body(): features = layer_norm(combined, out_gain[layer_index]).astype(jnp.bfloat16)]
    all_to_all x3 -> x0, starting transfers between devices: 21.3 us -> none  [the longest x1 10.7 us: body(): lax.all_to_all(pooled, ('dp', 'fsdp'), split_axis=0, concat_axis=1, tiled...]
    all_to_all x2 -> x0, local copies, waits for them, and re-layouts: 18.1 us -> none  [body(): lax.all_to_all(pooled, ('dp', 'fsdp'), split_axis=0, concat_axis=1, tiled...]
  transfers between devices with their start and end apart: 5 -> 0, of which waited for: 3 -> 0; matrix products, arithmetic and copies ran while one was open for 6% -> 0% of each run, Pallas kernels for 0% -> 0%
where the time goes in v1:
time: 389 us; the launch traced here: 387 us
  Pallas kernels  378 us (97%)
  local copies, waits for them, and re-layouts  7.32 us (2%)
    pallas_call x1, Pallas kernels, gather(): pl.pallas_call(gather_kernel, out_shape=(jax.ShapeDtypeStruct((BLOCK, N,...  247 us
    pallas_call x1, Pallas kernels, layers(): pl.pallas_call(layers_kernel, out_shape=jax.ShapeDtypeStruct((BLOCK, N, D...  131 us

profile of v1, /device:TPU:32, one launch (start us, length us, event | category | flops | bytes accessed | tf_op | source)
XLA Modules:
  0.0 386.6 jit_solution(16572929211978195441)
XLA Ops:
  0.0 1.7 pad_maximum_fusion.mixer
  1.7 0.9 reshape.14
  2.6 0.7 copy.9
  3.3 5.7 %copy.11 = bf16[2,256,16,256]{3,1,2,0:T(8,128)(2,1)} copy(bf16[2,256,16,256]{3,2,1,0:T(8,128)(2,1)} %bitcast.9) | data formatting | bytes 8388608 | tf_op jit(solution)/shard_map/reshape | solution.py:357
  9.0 246.5 %shard_map.73 = (bf16[128,256,128]{2,1,0:T(8,128)(2,1)}, bf16[2,16,256,2048]{3,2,1,0:T(8,128)(2,1)}) custom-call(bf16[16384,2,128]{2,1,0:T(2,128)(2,1)} %rows.1, bf16[2,16,256,256]{3,2,1,0:T(8,128)(2,1)} %bitcast.8), custom_call_target="tpu_custom_call" | custom-call | tf_op jit(solution)/shard_map/pallas_call | solution.py:212
  255.5 131.0 %shard_map.74 = bf16[128,256,128]{2,1,0:T(8,128)(2,1)} custom-call(bf16[128,256,128]{2,1,0:T(8,128)(2,1)} %get-tuple-element.7.x, bf16[2,16,256,2048]{3,2,1,0:T(8,128)(2,1)} %get-tuple-element.8.full, s32[1,256]{1,0:T(1,128)} %bitcast.12, bf16[2,256,256]{2,1,0:T(8,128)(2,1)} %pad_maximum_fusion.mixer, f32[2,16,256]{2,1,0:T(8,128)} %bitcast.10, ...), custom_call_target="tpu_custom_call" | custom-call | tf_op jit(solution)/shard_map/pallas_call | solution.py:340

commit v2 on v0

v2 whole, which is shorter than its diff:
```python
import jax
import jax.numpy as jnp
from jax import lax
from jax.experimental import pallas as pl
from jax.experimental.pallas import tpu as pltpu
from jax.sharding import PartitionSpec as P

N = 256
D = 128
K = 16
LAYERS = 2
DEVICES = 128
BLOCK = 128
CHUNKS = 4
STEP = BLOCK // CHUNKS
HALF = K // 2
MESH = pl.DeviceIdType.MESH
F32 = jnp.float32
BF16 = jnp.bfloat16


def position():
    dp, fsdp = lax.axis_index("dp"), lax.axis_index("fsdp")
    y, z_hi, core = dp // 4, lax.rem(dp // 2, 2), lax.rem(dp, 2)
    z_lo, x = fsdp // 4, lax.rem(fsdp, 4)
    return x, y, z_hi * 2 + z_lo, core


def device_at(x, y, z, core):
    x, y, z = lax.rem(x + 4, 4), lax.rem(y + 4, 4), lax.rem(z + 4, 4)
    return {"dp": (y * 2 + z // 2) * 2 + core, "fsdp": lax.rem(z, 2) * 4 + x}


def normalized(values, gain):
    center = jnp.mean(values, axis=-1, keepdims=True)
    apart = values - center
    spread = jnp.mean(apart * apart, axis=-1, keepdims=True)
    return (apart * lax.rsqrt(spread + 1e-05) * gain).astype(BF16)


def features_of_block(start, count, block, order, weights, layer, mixer, gains, out_gain, inter, fm):
    def pair(i, carry):
        a = start + 2 * i
        both = jnp.concatenate([block[a], block[a + 1]], axis=1)
        if order is not None:
            both = jnp.dot(order[...], both, preferred_element_type=F32).astype(BF16)
        mixed = jnp.dot(mixer[layer], both, preferred_element_type=F32)
        projected = mixed[:K].astype(BF16)
        none = jnp.zeros((K, D), BF16)
        apart = jnp.concatenate(
            [
                jnp.concatenate([projected[:, :D], none], axis=1),
                jnp.concatenate([none, projected[:, D:]], axis=1),
            ],
            axis=0,
        )
        products = lax.dot_general(
            apart, both, (((1,), (1,)), ((), ())), preferred_element_type=F32
        )
        for half in range(2):
            inter[half, pl.ds(pl.multiple_of(2 * i * K, 2 * K), 2 * K), :] = products[
                :, half * D : (half + 1) * D
            ]
        for s, at in ((a, 0), (a + 1, D)):
            rows = both[:, at : at + D]
            combined = mixed[K:, at : at + D] + rows[K:].astype(F32)
            block[s, :K] = rows[:K]
            block[s, K:] = normalized(combined, out_gain[layer])
        return carry

    lax.fori_loop(0, count // 2, pair, 0, unroll=8)

    def taken(k):
        return jnp.concatenate(
            [inter[half, pl.ds(k, count, stride=K), :] for half in range(2)], axis=1
        )

    total = jnp.zeros((count, N), F32)
    for k in range(K):
        total += taken(k)
    center = jnp.sum(total, axis=-1, keepdims=True) * (1.0 / (N * K))
    squares = jnp.zeros((count, N), F32)
    for k in range(K):
        apart = taken(k) - center
        squares += apart * apart
    scale = lax.rsqrt(jnp.sum(squares, axis=-1, keepdims=True) * (1.0 / (N * K)) + 1e-05)
    width = 1024

    def columns(j, carry):
        at = pl.multiple_of(j * width, width)
        made = jnp.zeros((count, width), F32)
        for k in range(K):
            apart = taken(k) - center
            normed = (apart * scale * gains[layer, k : k + 1, :]).astype(BF16)
            made += jnp.dot(
                normed, weights[layer, k, :, pl.ds(at, width)], preferred_element_type=F32
            )
        made = made.astype(BF16).astype(F32)
        for f in range(width // D):
            fm[pl.ds(j * (width // D) + f, count, stride=K), :] = made[:, f * D : (f + 1) * D]
        return carry

    lax.fori_loop(0, 2048 // width, columns, 0)

    def finish(s, carry):
        combined = fm[pl.ds(pl.multiple_of(s * K, K), K), :] + block[start + s, :K].astype(F32)
        block[start + s, :K] = normalized(combined, out_gain[layer])
        return carry

    lax.fori_loop(0, count, finish, 0, unroll=16)


def kernel(
    rows,
    shard,
    slots,
    mixer,
    gains,
    out_gain,
    out,
    block,
    full,
    order,
    inter,
    fm,
    send,
    arrive,
    w_send,
    w_arrive,
    own,
    w_own,
    leave,
):
    dp, fsdp = lax.axis_index("dp"), lax.axis_index("fsdp")
    me = dp * 8 + fsdp
    x, y, z, core = position()
    z_lo = lax.rem(z, 2)
    barrier = pltpu.get_barrier_semaphore()

    def mesh_of(t):
        return {"dp": t // 8, "fsdp": lax.rem(t, 8)}

    def greet(i, carry):
        pl.semaphore_signal(
            barrier, inc=1, device_id=mesh_of(lax.rem(me + i, DEVICES)), device_id_type=MESH
        )
        return carry

    lax.fori_loop(1, DEVICES, greet, 0)

    base = core * HALF
    five, three = pl.ds(base, 5), pl.ds(base + 5, 3)
    quarter = y * 64
    top, bottom = pl.ds(0, 128), pl.ds(128, 128)

    def part(at, size):
        return pl.ds(pl.multiple_of(at, size), size)

    def cols(i):
        return part(i * 256, 256)

    own_copies = []
    for layer in range(LAYERS):
        for j, (slabs, lines) in enumerate(((five, pl.ds(0, N)), (three, part(quarter, 64)))):
            copy = pltpu.make_async_copy(
                shard.at[layer, slabs, lines],
                full.at[layer, slabs, lines, cols(fsdp)],
                w_own.at[layer, j],
            )
            copy.start()
            own_copies.append(copy)
    order[...] = jnp.where(
        lax.broadcasted_iota(jnp.int32, (N, N), 0) == slots[...], 1.0, 0.0
    ).astype(BF16)
    pl.semaphore_wait(barrier, DEVICES - 1)
    sent = []

    def push(layer, slot, source, target, device):
        copy = pltpu.make_async_remote_copy(
            src_ref=source,
            dst_ref=target,
            send_sem=w_send.at[layer, slot],
            recv_sem=w_arrive.at[layer, slot],
            device_id=device,
            device_id_type=MESH,
        )
        copy.start()
        sent.append(copy)
        return copy

    def same(layer, slot, block, device):
        return push(layer, slot, block, block, device)

    right = device_at(x + 1, y, z, core)
    left = device_at(x - 1, y, z, core)
    z_up = device_at(x, y, z + 1, core)
    z_down = device_at(x, y, z - 1, core)
    y_up = device_at(x, y + 1, z, core)
    y_down = device_at(x, y - 1, z, core)
    sibling = device_at(x, y, z, 1 - core)
    x_left, x_right = lax.rem(x + 3, 4), lax.rem(x + 1, 4)
    y_lower, y_upper = lax.rem(y + 3, 4), lax.rem(y + 1, 4)

    def b_x1(layer):
        source, target = shard.at[layer, five], full.at[layer, five, :, cols(fsdp)]
        return [push(layer, 0, source, target, right), push(layer, 1, source, target, left)]

    def a_z(layer):
        return [
            push(
                layer,
                2 + j,
                shard.at[layer, three, part(quarter + 32 * j, 32)],
                full.at[layer, three, part(quarter + 32 * j, 32), cols(fsdp)],
                device,
            )
            for j, device in enumerate((z_up, z_down))
        ]

    def b_x2(layer):
        return [
            same(layer, 4, full.at[layer, five, top, cols(z_lo * 4 + x_left)], right),
            same(layer, 5, full.at[layer, five, bottom, cols(z_lo * 4 + x_right)], left),
        ]

    def a_x1(layer):
        return [
            same(layer, 6 + 2 * j + i, full.at[layer, three, part(quarter, 64), cols(4 * i + x)], device)
            for j, device in enumerate((right, left))
            for i in range(2)
        ]

    def b_z(layer):
        group = part(z_lo * 1024, 1024)
        return [
            same(layer, 10, full.at[layer, five, top, group], z_up),
            same(layer, 11, full.at[layer, five, bottom, group], z_down),
        ]

    def a_x2(layer):
        return [
            same(
                layer,
                12 + 2 * j + i,
                full.at[layer, three, part(quarter + 32 * j, 32), cols(4 * i + origin)],
                device,
            )
            for j, (device, origin) in enumerate(((right, x_left), (left, x_right)))
            for i in range(2)
        ]

    def a_y1(layer):
        lines = full.at[layer, three, part(quarter, 64)]
        return [same(layer, 16, lines, y_up), same(layer, 17, lines, y_down)]

    def b_core(layer):
        return [same(layer, 18, full.at[layer, five], sibling)]

    def a_y2(layer):
        return [
            same(layer, 19, full.at[layer, three, part(y_lower * 64, 32)], y_up),
            same(layer, 20, full.at[layer, three, part(y_upper * 64 + 32, 32)], y_down),
        ]

    def a_core(layer):
        return [same(layer, 21, full.at[layer, three], sibling)]

    def exchange(c):
        def send_one(i, carry):
            t = lax.rem(me + i, DEVICES)
            pltpu.make_async_remote_copy(
                src_ref=rows.at[pl.ds(t * BLOCK + c * STEP, STEP)],
                dst_ref=block.at[pl.ds(c * STEP, STEP), pl.ds(pl.multiple_of(2 * me, 2), 2)],
                send_sem=send.at[c],
                recv_sem=arrive.at[c],
                device_id=mesh_of(t),
                device_id_type=MESH,
            ).start()
            return carry

        lax.fori_loop(1, DEVICES, send_one, 0)
        pltpu.make_async_copy(
            rows.at[pl.ds(me * BLOCK + c * STEP, STEP)],
            block.at[pl.ds(c * STEP, STEP), pl.ds(pl.multiple_of(2 * me, 2), 2)],
            own.at[c],
        ).start()

    def arrived(copies):
        for copy in copies:
            copy.wait_recv()

    def start(layer):
        return b_x1(layer), a_z(layer)

    def spread(layer, b, a):
        arrived(a)
        a = a_x1(layer)
        arrived(b)
        return b_x2(layer), a

    def turn(layer, b, a):
        arrived(a)
        a = a_x2(layer)
        arrived(b)
        b = b_z(layer)
        arrived(a)
        return b, a_y1(layer)

    def close(layer, b, a):
        arrived(b)
        b = b_core(layer)
        arrived(a)
        return b, a_y2(layer)

    zero = start(0)
    for copy in own_copies:
        copy.wait()
    exchange(0)
    zero = spread(0, *zero)
    one = start(1)
    zero = turn(0, *zero)
    exchange(1)
    one = spread(1, *one)
    zero = close(0, *zero)
    one = turn(1, *one)
    exchange(2)
    arrived(zero[1])
    zero = zero[0] + a_core(0)
    one = close(1, *one)
    exchange(3)
    arrived(one[1])
    one = one[0] + a_core(1)
    arrived(zero)
    arrived(one)

    def step(c, carry):
        here = pl.ds(c * STEP, STEP)
        pltpu.make_async_copy(
            rows.at[pl.ds(0, STEP)], block.at[here, pl.ds(0, 2)], own.at[c]
        ).wait()
        others = block.at[here, pl.ds(0, N - 2)]
        pltpu.make_async_copy(others, others, arrive.at[c]).wait()
        for layer in range(LAYERS):
            features_of_block(
                c * STEP,
                STEP,
                block,
                order if layer == 0 else None,
                full,
                layer,
                mixer,
                gains,
                out_gain,
                inter,
                fm,
            )
        pltpu.make_async_copy(block.at[here], out.at[here], leave.at[c]).start()
        return carry

    lax.fori_loop(0, CHUNKS, step, 0)
    for c in range(CHUNKS):
        here = pl.ds(c * STEP, STEP)
        pltpu.make_async_copy(block.at[here], out.at[here], leave.at[c]).wait()
        others = block.at[here, pl.ds(0, N - 2)]
        pltpu.make_async_copy(others, others, send.at[c]).wait()
    for copy in sent:
        copy.wait_send()


def layers(rows, shard, slots, mixer, gains, out_gain):
    vmem = pl.BlockSpec(memory_space=pltpu.VMEM)
    hbm = pl.BlockSpec(memory_space=pl.ANY)
    pushes = 22
    return pl.pallas_call(
        kernel,
        out_shape=jax.ShapeDtypeStruct((BLOCK, N, D), BF16),
        in_specs=[hbm, hbm, vmem, vmem, vmem, vmem],
        out_specs=hbm,
        scratch_shapes=[
            pltpu.VMEM((BLOCK, N, D), BF16),
            pltpu.VMEM((LAYERS, K, N, 2048), BF16),
            pltpu.VMEM((N, N), BF16),
            pltpu.VMEM((2, STEP * K, D), F32),
            pltpu.VMEM((STEP * K, D), F32),
            pltpu.SemaphoreType.DMA((CHUNKS,)),
            pltpu.SemaphoreType.DMA((CHUNKS,)),
            pltpu.SemaphoreType.DMA((LAYERS, pushes)),
            pltpu.SemaphoreType.DMA((LAYERS, pushes)),
            pltpu.SemaphoreType.DMA((CHUNKS,)),
            pltpu.SemaphoreType.DMA((LAYERS, 2)),
            pltpu.SemaphoreType.DMA((CHUNKS,)),
        ],
        compiler_params=pltpu.CompilerParams(
            collective_id=0, has_side_effects=True, vmem_limit_bytes=60 << 20
        ),
    )(rows, shard, slots, mixer, gains, out_gain)


def body(pooled, feature_order, fm_proj, fm_gain, mlp_weight, lcb_weight, out_gain):
    shard = mlp_weight.reshape(LAYERS, N, K, 256).transpose(0, 2, 1, 3)
    gains = fm_gain.reshape(LAYERS, N, K).transpose(0, 2, 1)
    mixer = jnp.concatenate([fm_proj.transpose(0, 2, 1), lcb_weight], axis=1)
    return layers(
        pooled, shard, feature_order.reshape(1, N), mixer, gains, out_gain.reshape(LAYERS, 1, D)
    )


def solution(mesh):
    placed = (P(None, ("dp", "fsdp"), None), P(), P(), P(), P(None, None, "fsdp"), P(), P())
    return jax.shard_map(
        body, mesh=mesh, in_specs=placed, out_specs=P(("dp", "fsdp"), None, None), check_vma=False
    )
```

time: 542 us -> 290 us (0.54)
  the two profiles are of different devices: /device:TPU:32 before, /device:TPU:57 now
where the time goes in v2:
time: 290 us
  Pallas kernels  273 us (94%)
  local copies, waits for them, and re-layouts  15.2 us (5%)
    pallas_call x1, Pallas kernels, layers(): pl.pallas_call(kernel, out_shape=jax.ShapeDtypeStruct((BLOCK, N, D), BF16...  273 us
    unnamed x1, local copies, waits for them, and re-layouts  7.89 us

profile of v2, /device:TPU:57, one launch (start us, length us, event | category | flops | bytes accessed | tf_op | source)
XLA Modules:
  0.0 289.8 jit_solution(12272777789370294778)
XLA Ops:
  0.0 1.7 pad_maximum_fusion.mixer
  1.7 0.9 reshape.14
  2.6 0.7 copy.9
  3.3 5.7 %copy.11 = bf16[2,256,16,256]{3,1,2,0:T(8,128)(2,1)} copy(bf16[2,256,16,256]{3,2,1,0:T(8,128)(2,1)} %bitcast.9) | data formatting | bytes 8388608 | tf_op jit(solution)/shard_map/reshape | solution.py:400
  9.0 272.9 %shard_map.73 = bf16[128,256,128]{2,1,0:T(8,128)(2,1)} custom-call(bf16[16384,2,128]{2,1,0:T(2,128)(2,1)} %rows.1, bf16[2,16,256,256]{3,2,1,0:T(8,128)(2,1)} %bitcast.8, s32[1,256]{1,0:T(1,128)} %bitcast.12, bf16[2,256,256]{2,1,0:T(8,128)(2,1)} %pad_maximum_fusion.mixer, f32[2,16,256]{2,1,0:T(8,128)} %bitcast.10, f32[2,1,128]{2,1,0:T(1,128)} %bitcast.13), custom_call_target="tpu_custom_call" | custom-call | tf_op jit(solution)/shard_map/pallas_call | solution.py:374
  281.9 7.9 %copy.13 = bf16[128,256,128]{2,1,0:T(8,128)(2,1)} copy(bf16[128,256,128]{2,1,0:T(8,128)(2,1)} %shard_map.73) | data formatting | bytes 16777216

commit v3 on v2

--- a/solution.py
+++ b/solution.py
@@ -14,6 +14,8 @@
 CHUNKS = 4
 STEP = BLOCK // CHUNKS
 HALF = K // 2
+PIECES = 4
+PUSHES = 160
 MESH = pl.DeviceIdType.MESH
 F32 = jnp.float32
 BF16 = jnp.bfloat16
@@ -175,12 +177,12 @@
     pl.semaphore_wait(barrier, DEVICES - 1)
     sent = []
 
-    def push(layer, slot, source, target, device):
+    def push(source, target, device):
         copy = pltpu.make_async_remote_copy(
             src_ref=source,
             dst_ref=target,
-            send_sem=w_send.at[layer, slot],
-            recv_sem=w_arrive.at[layer, slot],
+            send_sem=w_send.at[len(sent)],
+            recv_sem=w_arrive.at[len(sent)],
             device_id=device,
             device_id_type=MESH,
         )
@@ -188,8 +190,8 @@
         sent.append(copy)
         return copy
 
-    def same(layer, slot, block, device):
-        return push(layer, slot, block, block, device)
+    def same(block, device):
+        return push(block, block, device)
 
     right = device_at(x + 1, y, z, core)
     left = device_at(x - 1, y, z, core)
@@ -201,73 +203,54 @@
     x_left, x_right = lax.rem(x + 3, 4), lax.rem(x + 1, 4)
     y_lower, y_upper = lax.rem(y + 3, 4), lax.rem(y + 1, 4)
 
-    def b_x1(layer):
-        source, target = shard.at[layer, five], full.at[layer, five, :, cols(fsdp)]
-        return [push(layer, 0, source, target, right), push(layer, 1, source, target, left)]
-
-    def a_z(layer):
-        return [
+    quarter_halves = [part(quarter + 32 * j, 32) for j in range(2)]
+    group = part(z_lo * 1024, 1024)
+
+    def along_x_z(layer, slab):
+        source, target = shard.at[layer, slab], full.at[layer, slab, :, cols(fsdp)]
+        yield [push(source, target, right), push(source, target, left)]
+        yield [
+            same(full.at[layer, slab, top, cols(z_lo * 4 + x_left)], right),
+            same(full.at[layer, slab, bottom, cols(z_lo * 4 + x_right)], left),
+        ]
+        yield [
+            same(full.at[layer, slab, top, group], z_up),
+            same(full.at[layer, slab, bottom, group], z_down),
+        ]
+        yield [same(full.at[layer, slab], sibling)]
+
+    def along_z_x_y(layer, slab):
+        yield [
             push(
-                layer,
-                2 + j,
-                shard.at[layer, three, part(quarter + 32 * j, 32)],
-                full.at[layer, three, part(quarter + 32 * j, 32), cols(fsdp)],
+                shard.at[layer, slab, quarter_halves[j]],
+                full.at[layer, slab, quarter_halves[j], cols(fsdp)],
                 device,
             )
             for j, device in enumerate((z_up, z_down))
         ]
-
-    def b_x2(layer):
-        return [
-            same(layer, 4, full.at[layer, five, top, cols(z_lo * 4 + x_left)], right),
-            same(layer, 5, full.at[layer, five, bottom, cols(z_lo * 4 + x_right)], left),
-        ]
-
-    def a_x1(layer):
-        return [
-            same(layer, 6 + 2 * j + i, full.at[layer, three, part(quarter, 64), cols(4 * i + x)], device)
-            for j, device in enumerate((right, left))
+        yield [
+            same(full.at[layer, slab, part(quarter, 64), cols(4 * i + x)], device)
+            for device in (right, left)
             for i in range(2)
         ]
-
-    def b_z(layer):
-        group = part(z_lo * 1024, 1024)
-        return [
-            same(layer, 10, full.at[layer, five, top, group], z_up),
-            same(layer, 11, full.at[layer, five, bottom, group], z_down),
-        ]
-
-    def a_x2(layer):
-        return [
-            same(
-                layer,
-                12 + 2 * j + i,
-                full.at[layer, three, part(quarter + 32 * j, 32), cols(4 * i + origin)],
-                device,
-            )
+        yield [
+            same(full.at[layer, slab, quarter_halves[j], cols(4 * i + origin)], device)
             for j, (device, origin) in enumerate(((right, x_left), (left, x_right)))
             for i in range(2)
         ]
-
-    def a_y1(layer):
-        lines = full.at[layer, three, part(quarter, 64)]
-        return [same(layer, 16, lines, y_up), same(layer, 17, lines, y_down)]
-
-    def b_core(layer):
-        return [same(layer, 18, full.at[layer, five], sibling)]
-
-    def a_y2(layer):
-        return [
-            same(layer, 19, full.at[layer, three, part(y_lower * 64, 32)], y_up),
-            same(layer, 20, full.at[layer, three, part(y_upper * 64 + 32, 32)], y_down),
-        ]
-
-    def a_core(layer):
-        return [same(layer, 21, full.at[layer, three], sibling)]
-
-    def exchange(c):
+        lines = full.at[layer, slab, part(quarter, 64)]
+        yield [same(lines, y_up), same(lines, y_down)]
+        yield [
+            same(full.at[layer, slab, part(y_lower * 64, 32)], y_up),
+            same(full.at[layer, slab, part(y_upper * 64 + 32, 32)], y_down),
+        ]
+        yield [same(full.at[layer, slab], sibling)]
+
+    def exchange(piece):
+        c, first = piece // PIECES, piece % PIECES * (DEVICES // PIECES)
+
         def send_one(i, carry):
-            t = lax.rem(me + i, DEVICES)
+            t = lax.rem(me + i * 37, DEVICES)
             pltpu.make_async_remote_copy(
                 src_ref=rows.at[pl.ds(t * BLOCK + c * STEP, STEP)],
                 dst_ref=block.at[pl.ds(c * STEP, STEP), pl.ds(pl.multiple_of(2 * me, 2), 2)],
@@ -278,60 +261,41 @@
             ).start()
             return carry
 
-        lax.fori_loop(1, DEVICES, send_one, 0)
-        pltpu.make_async_copy(
-            rows.at[pl.ds(me * BLOCK + c * STEP, STEP)],
-            block.at[pl.ds(c * STEP, STEP), pl.ds(pl.multiple_of(2 * me, 2), 2)],
-            own.at[c],
-        ).start()
-
-    def arrived(copies):
-        for copy in copies:
-            copy.wait_recv()
-
-    def start(layer):
-        return b_x1(layer), a_z(layer)
-
-    def spread(layer, b, a):
-        arrived(a)
-        a = a_x1(layer)
-        arrived(b)
-        return b_x2(layer), a
-
-    def turn(layer, b, a):
-        arrived(a)
-        a = a_x2(layer)
-        arrived(b)
-        b = b_z(layer)
-        arrived(a)
-        return b, a_y1(layer)
-
-    def close(layer, b, a):
-        arrived(b)
-        b = b_core(layer)
-        arrived(a)
-        return b, a_y2(layer)
-
-    zero = start(0)
-    for copy in own_copies:
-        copy.wait()
-    exchange(0)
-    zero = spread(0, *zero)
-    one = start(1)
-    zero = turn(0, *zero)
-    exchange(1)
-    one = spread(1, *one)
-    zero = close(0, *zero)
-    one = turn(1, *one)
-    exchange(2)
-    arrived(zero[1])
-    zero = zero[0] + a_core(0)
-    one = close(1, *one)
-    exchange(3)
-    arrived(one[1])
-    one = one[0] + a_core(1)
-    arrived(zero)
-    arrived(one)
+        lax.fori_loop(max(first, 1), first + DEVICES // PIECES, send_one, 0)
+        if first == 0:
+            pltpu.make_async_copy(
+                rows.at[pl.ds(me * BLOCK + c * STEP, STEP)],
+                block.at[pl.ds(c * STEP, STEP), pl.ds(pl.multiple_of(2 * me, 2), 2)],
+                own.at[c],
+            ).start()
+
+    ways = []
+    for layer in range(LAYERS):
+        for i in range(5):
+            ways.append([layer * 5 + i, along_x_z(layer, base + i), []])
+        for i in range(3):
+            ways.append([layer * 3 + i, along_z_x_y(layer, base + 5 + i), []])
+    ways.sort(key=lambda way: way[0])
+    pieces = CHUNKS * PIECES
+    ticks, issued = 0, 0
+    while ways:
+        for way in ways:
+            if way[0] <= ticks and (ticks - way[0]) % 2 == 0:
+                for copy in way[2]:
+                    copy.wait_recv()
+                way[2] = next(way[1], None)
+        ways = [way for way in ways if way[2] is not None]
+        if ticks == 0:
+            for copy in own_copies:
+                copy.wait()
+        wanted = min(pieces, (ticks + 1) // 2)
+        while issued < wanted:
+            exchange(issued)
+            issued += 1
+        ticks += 1
+    while issued < pieces:
+        exchange(issued)
+        issued += 1
 
     def step(c, carry):
         here = pl.ds(c * STEP, STEP)
@@ -370,7 +334,6 @@
 def layers(rows, shard, slots, mixer, gains, out_gain):
     vmem = pl.BlockSpec(memory_space=pltpu.VMEM)
     hbm = pl.BlockSpec(memory_space=pl.ANY)
-    pushes = 22
     return pl.pallas_call(
         kernel,
         out_shape=jax.ShapeDtypeStruct((BLOCK, N, D), BF16),
@@ -384,8 +347,8 @@
             pltpu.VMEM((STEP * K, D), F32),
             pltpu.SemaphoreType.DMA((CHUNKS,)),
             pltpu.SemaphoreType.DMA((CHUNKS,)),
-            pltpu.SemaphoreType.DMA((LAYERS, pushes)),
-            pltpu.SemaphoreType.DMA((LAYERS, pushes)),
+            pltpu.SemaphoreType.DMA((PUSHES,)),
+            pltpu.SemaphoreType.DMA((PUSHES,)),
             pltpu.SemaphoreType.DMA((CHUNKS,)),
             pltpu.SemaphoreType.DMA((LAYERS, 2)),
             pltpu.SemaphoreType.DMA((CHUNKS,)),

time: 290 us -> 220 us (0.76)
  the two profiles are of different devices: /device:TPU:57 before, /device:TPU:32 now
where the time goes in v3:
time: 220 us
  Pallas kernels  203 us (92%)
  local copies, waits for them, and re-layouts  15.2 us (7%)
    pallas_call x1, Pallas kernels, layers(): pl.pallas_call(kernel, out_shape=jax.ShapeDtypeStruct((BLOCK, N, D), BF16...  203 us
    unnamed x1, local copies, waits for them, and re-layouts  7.89 us
    reshape x1, local copies, waits for them, and re-layouts, body(): shard = mlp_weight.reshape(LAYERS, N, K, 256).transpose(0, 2, 1, 3)  5.72 us

profile of v3, /device:TPU:32, one launch (start us, length us, event | category | flops | bytes accessed | tf_op | source)
XLA Modules:
  0.0 219.6 jit_solution(11614620604852400162)
XLA Ops:
  0.0 1.7 pad_maximum_fusion.mixer
  1.7 0.9 reshape.14
  2.6 0.7 copy.9
  3.3 5.7 %copy.11 = bf16[2,256,16,256]{3,1,2,0:T(8,128)(2,1)} copy(bf16[2,256,16,256]{3,2,1,0:T(8,128)(2,1)} %bitcast.9) | data formatting | bytes 8388608 | tf_op jit(solution)/shard_map/reshape | solution.py:363
  9.0 202.7 %shard_map.73 = bf16[128,256,128]{2,1,0:T(8,128)(2,1)} custom-call(bf16[16384,2,128]{2,1,0:T(2,128)(2,1)} %rows.1, bf16[2,16,256,256]{3,2,1,0:T(8,128)(2,1)} %bitcast.8, s32[1,256]{1,0:T(1,128)} %bitcast.12, bf16[2,256,256]{2,1,0:T(8,128)(2,1)} %pad_maximum_fusion.mixer, f32[2,16,256]{2,1,0:T(8,128)} %bitcast.10, f32[2,1,128]{2,1,0:T(1,128)} %bitcast.13), custom_call_target="tpu_custom_call" | custom-call | tf_op jit(solution)/shard_map/pallas_call | solution.py:337
  211.7 7.9 %copy.13 = bf16[128,256,128]{2,1,0:T(8,128)(2,1)} copy(bf16[128,256,128]{2,1,0:T(8,128)(2,1)} %shard_map.73) | data formatting | bytes 16777216

commit v4 on v3

--- a/solution.py
+++ b/solution.py
@@ -116,13 +116,15 @@
     rows,
     shard,
     slots,
-    mixer,
-    gains,
+    fm_proj,
+    lcb_weight,
+    fm_gain,
     out_gain,
-    out,
     block,
     full,
     order,
+    mixer,
+    gains,
     inter,
     fm,
     send,
@@ -131,7 +133,6 @@
     w_arrive,
     own,
     w_own,
-    leave,
 ):
     dp, fsdp = lax.axis_index("dp"), lax.axis_index("fsdp")
     me = dp * 8 + fsdp
@@ -288,6 +289,10 @@
         if ticks == 0:
             for copy in own_copies:
                 copy.wait()
+            for layer in range(LAYERS):
+                mixer[layer, :K] = fm_proj[layer]
+                mixer[layer, K:] = lcb_weight[layer]
+                gains[layer] = fm_gain[layer].T
         wanted = min(pieces, (ticks + 1) // 2)
         while issued < wanted:
             exchange(issued)
@@ -318,31 +323,30 @@
                 inter,
                 fm,
             )
-        pltpu.make_async_copy(block.at[here], out.at[here], leave.at[c]).start()
         return carry
 
     lax.fori_loop(0, CHUNKS, step, 0)
     for c in range(CHUNKS):
         here = pl.ds(c * STEP, STEP)
-        pltpu.make_async_copy(block.at[here], out.at[here], leave.at[c]).wait()
         others = block.at[here, pl.ds(0, N - 2)]
         pltpu.make_async_copy(others, others, send.at[c]).wait()
     for copy in sent:
         copy.wait_send()
 
 
-def layers(rows, shard, slots, mixer, gains, out_gain):
+def layers(rows, shard, slots, fm_proj, lcb_weight, fm_gain, out_gain):
     vmem = pl.BlockSpec(memory_space=pltpu.VMEM)
     hbm = pl.BlockSpec(memory_space=pl.ANY)
     return pl.pallas_call(
         kernel,
-        out_shape=jax.ShapeDtypeStruct((BLOCK, N, D), BF16),
-        in_specs=[hbm, hbm, vmem, vmem, vmem, vmem],
-        out_specs=hbm,
+        out_shape=pltpu.VMEM((BLOCK, N, D), BF16),
+        in_specs=[hbm, hbm, vmem, vmem, vmem, vmem, vmem],
+        out_specs=vmem,
         scratch_shapes=[
-            pltpu.VMEM((BLOCK, N, D), BF16),
             pltpu.VMEM((LAYERS, K, N, 2048), BF16),
             pltpu.VMEM((N, N), BF16),
+            pltpu.VMEM((LAYERS, N, N), BF16),
+            pltpu.VMEM((LAYERS, K, N), F32),
             pltpu.VMEM((2, STEP * K, D), F32),
             pltpu.VMEM((STEP * K, D), F32),
             pltpu.SemaphoreType.DMA((CHUNKS,)),
@@ -351,21 +355,20 @@
             pltpu.SemaphoreType.DMA((PUSHES,)),
             pltpu.SemaphoreType.DMA((CHUNKS,)),
             pltpu.SemaphoreType.DMA((LAYERS, 2)),
-            pltpu.SemaphoreType.DMA((CHUNKS,)),
         ],
         compiler_params=pltpu.CompilerParams(
-            collective_id=0, has_side_effects=True, vmem_limit_bytes=60 << 20
+            collective_id=0, has_side_effects=True, vmem_limit_bytes=40 << 20
         ),
-    )(rows, shard, slots, mixer, gains, out_gain)
+    )(rows, shard, slots, fm_proj, lcb_weight, fm_gain, out_gain)
 
 
 def body(pooled, feature_order, fm_proj, fm_gain, mlp_weight, lcb_weight, out_gain):
     shard = mlp_weight.reshape(LAYERS, N, K, 256).transpose(0, 2, 1, 3)
-    gains = fm_gain.reshape(LAYERS, N, K).transpose(0, 2, 1)
-    mixer = jnp.concatenate([fm_proj.transpose(0, 2, 1), lcb_weight], axis=1)
-    return layers(
-        pooled, shard, feature_order.reshape(1, N), mixer, gains, out_gain.reshape(LAYERS, 1, D)
-    )
+    gains = fm_gain.reshape(LAYERS, N, K)
+    slots = feature_order.reshape(1, N)
+    out_gains = out_gain.reshape(LAYERS, 1, D)
+    projections = fm_proj.transpose(0, 2, 1)
+    return layers(pooled, shard, slots, projections, lcb_weight, gains, out_gains)
 
 
 def solution(mesh):

time: 220 us -> 209 us (0.950)
  local copies, waits for them, and re-layouts: 15.2 us -> 8.06 us
    unnamed x1 -> x9, local copies, waits for them, and re-layouts: 7.89 us -> 3.41 us
where the time goes in v4:
time: 209 us
  Pallas kernels  201 us (96%)
  local copies, waits for them, and re-layouts  8.06 us (4%)
    pallas_call x1, Pallas kernels, layers(): pl.pallas_call(kernel, out_shape=pltpu.VMEM((BLOCK, N, D), BF16), in_spec...  201 us

profile of v4, /device:TPU:32, one launch (start us, length us, event | category | flops | bytes accessed | tf_op | source)
XLA Modules:
  0.0 209.0 jit_solution(14282561727866070312)
XLA Ops:
  0.0 0.0 copy-start.3
  0.0 0.0 copy-start
  0.0 0.0 copy-start.1
  0.0 0.0 copy-start.2
  0.0 0.9 reshape.14.fm_gain
  1.0 3.7 %copy.10 = bf16[2,256,16,256]{3,1,2,0:T(8,128)(2,1)S(1)} copy(bf16[2,256,16,256]{3,2,1,0:T(8,128)(2,1)} %bitcast.11) | data formatting | bytes 8388608 | tf_op jit(solution)/shard_map/reshape | solution.py:366
  4.7 0.0 copy-done.3
  4.7 0.0 copy-done
  4.7 0.0 copy-done.1
  4.7 0.0 copy-done.2
  4.7 200.9 %shard_map.73 = bf16[128,256,128]{2,1,0:T(8,128)(2,1)S(1)} custom-call(bf16[16384,2,128]{2,1,0:T(2,128)(2,1)} %rows.1, bf16[2,16,256,256]{3,2,1,0:T(8,128)(2,1)S(1)} %bitcast.7, s32[1,256]{1,0:T(1,128)S(1)} %bitcast.9, bf16[2,16,256]{2,1,0:T(8,128)(2,1)S(1)} %bitcast.8, bf16[2,240,256]{2,1,0:T(8,128)(2,1)S(1)} %copy-done, ...), custom_call_target="tpu_custom_call" | custom-call | tf_op jit(solution)/shard_map/pallas_call | solution.py:340
  205.6 3.4 %copy.12 = bf16[128,256,128]{2,1,0:T(8,128)(2,1)} copy(bf16[128,256,128]{2,1,0:T(8,128)(2,1)S(1)} %shard_map.73) | data formatting | bytes 16777216
Async XLA Ops:
  0.0 4.7 %copy-start.3 = (f32[2,128]{1,0:T(2,128)S(1)}, f32[2,128]{1,0:T(2,128)}, u32[]{:S(2)}) copy-start(f32[2,128]{1,0:T(2,128)} %param.13) | copy-start | bytes 3076
  0.0 4.7 %copy-start = (bf16[2,240,256]{2,1,0:T(8,128)(2,1)S(1)}, bf16[2,240,256]{2,1,0:T(8,128)(2,1)}, u32[]{:S(2)}) copy-start(bf16[2,240,256]{2,1,0:T(8,128)(2,1)} %lcb_weight.1) | copy-start | bytes 737284
  0.0 4.7 %copy-start.1 = (bf16[2,256,16]{1,2,0:T(8,128)(2,1)S(1)}, bf16[2,256,16]{1,2,0:T(8,128)(2,1)}, u32[]{:S(2)}) copy-start(bf16[2,256,16]{1,2,0:T(8,128)(2,1)} %param.9) | copy-start | bytes 49156
  0.0 4.7 %copy-start.2 = (s32[256]{0:T(256)S(1)}, s32[256]{0:T(256)}, u32[]{:S(2)}) copy-start(s32[256]{0:T(256)} %param.8) | copy-start | bytes 3076

commit v5 on v4

--- a/solution.py
+++ b/solution.py
@@ -164,9 +164,14 @@
 
     own_copies = []
     for layer in range(LAYERS):
-        for j, (slabs, lines) in enumerate(((five, pl.ds(0, N)), (three, part(quarter, 64)))):
+        for j, (taken, slabs, lines) in enumerate(
+            (
+                (pl.ds(0, 5), five, pl.ds(0, N)),
+                (pl.ds(5, 3), three, part(quarter, 64)),
+            )
+        ):
             copy = pltpu.make_async_copy(
-                shard.at[layer, slabs, lines],
+                shard.at[layer, taken, lines],
                 full.at[layer, slabs, lines, cols(fsdp)],
                 w_own.at[layer, j],
             )
@@ -208,7 +213,7 @@
     group = part(z_lo * 1024, 1024)
 
     def along_x_z(layer, slab):
-        source, target = shard.at[layer, slab], full.at[layer, slab, :, cols(fsdp)]
+        source, target = shard.at[layer, slab - base], full.at[layer, slab, :, cols(fsdp)]
         yield [push(source, target, right), push(source, target, left)]
         yield [
             same(full.at[layer, slab, top, cols(z_lo * 4 + x_left)], right),
@@ -223,7 +228,7 @@
     def along_z_x_y(layer, slab):
         yield [
             push(
-                shard.at[layer, slab, quarter_halves[j]],
+                shard.at[layer, slab - base, quarter_halves[j]],
                 full.at[layer, slab, quarter_halves[j], cols(fsdp)],
                 device,
             )
@@ -363,7 +368,9 @@
 
 
 def body(pooled, feature_order, fm_proj, fm_gain, mlp_weight, lcb_weight, out_gain):
-    shard = mlp_weight.reshape(LAYERS, N, K, 256).transpose(0, 2, 1, 3)
+    first = lax.rem(lax.axis_index("dp"), 2) * HALF
+    slabs = lax.dynamic_slice_in_dim(mlp_weight.reshape(LAYERS, N, K, 256), first, HALF, axis=2)
+    shard = slabs.transpose(0, 2, 1, 3)
     gains = fm_gain.reshape(LAYERS, N, K)
     slots = feature_order.reshape(1, N)
     out_gains = out_gain.reshape(LAYERS, 1, D)

time: 209 us -> 208 us (level)
    reshape x1 -> x0, local copies, waits for them, and re-layouts: 3.71 us -> none  [body(): shard = mlp_weight.reshape(LAYERS, N, K, 256).transpose(0, 2, 1, 3)]
where the time goes in v5:
time: 208 us; the launch traced here: 207 us
  Pallas kernels  201 us (97%)
  local copies, waits for them, and re-layouts  6.6 us (3%)
    pallas_call x1, Pallas kernels, layers(): pl.pallas_call(kernel, out_shape=pltpu.VMEM((BLOCK, N, D), BF16), in_spec...  201 us

profile of v5, /device:TPU:32, one launch (start us, length us, event | category | flops | bytes accessed | tf_op | source)
XLA Modules:
  0.0 207.5 jit_solution(10844730382537549955)
XLA Ops:
  0.0 0.9 reshape.14.fm_gain
  0.9 0.0 copy-start
  0.9 0.0 copy-start.1
  0.9 0.0 copy-start.2
  0.9 0.0 copy-start.3
  0.9 1.8 constant_dynamic-slice_fusion
  2.8 0.5 copy.11
  3.2 0.0 copy-done
  3.2 0.0 copy-done.1
  3.3 0.0 copy-done.2
  3.3 0.0 copy-done.3
  3.3 200.8 %shard_map.73 = bf16[128,256,128]{2,1,0:T(8,128)(2,1)S(1)} custom-call(bf16[16384,2,128]{2,1,0:T(2,128)(2,1)} %rows.1, bf16[2,8,256,256]{3,2,1,0:T(8,128)(2,1)S(1)} %bitcast.7, s32[1,256]{1,0:T(1,128)S(1)} %bitcast.9, bf16[2,16,256]{2,1,0:T(8,128)(2,1)S(1)} %bitcast.8, bf16[2,240,256]{2,1,0:T(8,128)(2,1)S(1)} %copy-done, f32[2,256,16]{2,1,0:T(8,128)S(1)} %reshape.14.fm_gain, ...), custom_call_target="tpu_custom_call" | custom-call | tf_op jit(solution)/shard_map/pallas_call | solution.py:345
  204.1 3.4 %copy.13 = bf16[128,256,128]{2,1,0:T(8,128)(2,1)} copy(bf16[128,256,128]{2,1,0:T(8,128)(2,1)S(1)} %shard_map.73) | data formatting | bytes 16777216
Async XLA Ops:
  0.9 2.3 %copy-start = (bf16[2,240,256]{2,1,0:T(8,128)(2,1)S(1)}, bf16[2,240,256]{2,1,0:T(8,128)(2,1)}, u32[]{:S(2)}) copy-start(bf16[2,240,256]{2,1,0:T(8,128)(2,1)} %lcb_weight.1) | copy-start | bytes 737284
  0.9 2.3 %copy-start.1 = (bf16[2,256,16]{1,2,0:T(8,128)(2,1)S(1)}, bf16[2,256,16]{1,2,0:T(8,128)(2,1)}, u32[]{:S(2)}) copy-start(bf16[2,256,16]{1,2,0:T(8,128)(2,1)} %param.9) | copy-start | bytes 49156
  0.9 2.3 %copy-start.2 = (s32[256]{0:T(256)S(1)}, s32[256]{0:T(256)}, u32[]{:S(2)}) copy-start(s32[256]{0:T(256)} %param.8) | copy-start | bytes 3076
  0.9 2.3 %copy-start.3 = (f32[2,128]{1,0:T(2,128)S(1)}, f32[2,128]{1,0:T(2,128)}, u32[]{:S(2)}) copy-start(f32[2,128]{1,0:T(2,128)} %param.13) | copy-start | bytes 3076
